TPU v7x, 32 devices: a whole 2x2x4 slice. The times are simulated.
32 devices in a mesh: cand: 8 (over y, x, core), ref: 4 (over z).
Axes of the slice: x: 2, y: 2, z: 4, core: 2. Of those that a mesh axis runs over, the one named last changes fastest.
Arguments:
- cand_factor: float32 [8192, 512], P('cand'), may hold values from -6 to 6
- ref_factor: float32 [2048, 512], P('ref'), may hold values from -6 to 6
- cand_plan: float32 [8192, 128], P('cand'), may hold values from 0.0625 to 16
- ref_plan: float32 [2048, 128], P('ref'), may hold values from 0.0625 to 16
- weights: float32 [128], replicated, may hold values from 0.5 to 2
Outputs:
- new_cand_plan: float32 [8192, 128], P('cand')
- new_ref_plan: float32 [2048, 128], P('ref')
- new_weights: float32 [128], replicated
All inputs are finite; a program needn't handle non-finite values. Where the computation divides by a largest or mean magnitude, that divisor is 1e-20 or more.
Results may differ from a plain program's by a relative error of at most 0.00019.
Values sent between devices are 32-bit elements; how exact they have to be, the bound alone decides.
No kernel may reach another device: no remote copies, remote signals or barrier semaphores. Data moves between devices by JAX's collectives and lax.ppermute only.
A program may use at most 64 MiB of HBM per device.

v0:
```python
import jax
import jax.numpy as jnp
from jax import lax
from jax.sharding import PartitionSpec as P

ITERS = 3
step_size = 3.0
tiny_value = 1e-06


def contract_rows(left, right):
    return lax.dot_general(
        left,
        right,
        (((0,), (0,)), ((), ())),
        precision=lax.Precision.HIGHEST,
        preferred_element_type=jnp.float32,
    )


def on_device(cand_factor, ref_factor, cand_plan, ref_plan, weights):
    cand_count = lax.axis_size("cand")
    ref_count = lax.axis_size("ref")
    cand_total = cand_factor.shape[0] * cand_count
    ref_total = ref_factor.shape[0] * ref_count
    rank_width = weights.shape[0]
    cand_block, cand_local = (cand_factor, cand_plan)
    ref_block, ref_local = (ref_factor, ref_plan)
    cand_partial = contract_rows(cand_block, cand_local) / cand_total
    ref_partial = contract_rows(ref_block, ref_local) / ref_total
    cand_moment = lax.psum(cand_partial, "cand")
    ref_moment = lax.psum(ref_partial, "ref")
    grad_cand = jnp.dot(cand_block, ref_moment, precision=lax.Precision.HIGHEST) / weights[None, :]
    grad_ref = jnp.dot(ref_block, cand_moment, precision=lax.Precision.HIGHEST) / weights[None, :]
    grad_weights = -jnp.sum(cand_moment * ref_moment, axis=0) / (weights * weights)
    local_top = jnp.maximum(jnp.max(jnp.abs(grad_cand)), jnp.max(jnp.abs(grad_ref)))
    global_top = lax.pmax(local_top, ("cand", "ref"))
    top = jnp.maximum(global_top, jnp.max(jnp.abs(grad_weights))) + tiny_value
    kernel_cand = cand_local * jnp.exp(-step_size * grad_cand / top)
    kernel_ref = ref_local * jnp.exp(-step_size * grad_ref / top)
    kernel_weights = weights * jnp.exp(-step_size * grad_weights / top)
    scale_cand = jnp.ones((rank_width,), jnp.float32)
    scale_ref = jnp.ones((rank_width,), jnp.float32)
    for repeat_index in range(ITERS):
        row_cand = rank_width / jnp.dot(kernel_cand, scale_cand, precision=lax.Precision.HIGHEST)
        row_ref = rank_width / jnp.dot(kernel_ref, scale_ref, precision=lax.Precision.HIGHEST)
        cand_mass_part = (
            jnp.dot(row_cand, kernel_cand, precision=lax.Precision.HIGHEST) / cand_total
        )
        ref_mass_part = jnp.dot(row_ref, kernel_ref, precision=lax.Precision.HIGHEST) / ref_total
        mass_cand = lax.psum(cand_mass_part, "cand")
        mass_ref = lax.psum(ref_mass_part, "ref")
        new_weights = jnp.cbrt(kernel_weights * scale_cand * mass_cand * scale_ref * mass_ref)
        scale_cand = new_weights / mass_cand
        scale_ref = new_weights / mass_ref
    new_cand_plan = row_cand[:, None] * kernel_cand * scale_cand[None, :]
    new_ref_plan = row_ref[:, None] * kernel_ref * scale_ref[None, :]
    return (new_cand_plan, new_ref_plan, new_weights)


def solution(mesh):
    in_specs = (P("cand", None), P("ref", None), P("cand", None), P("ref", None), P())
    out_specs = (P("cand", None), P("ref", None), P())
    return jax.shard_map(
        on_device, mesh=mesh, in_specs=in_specs, out_specs=out_specs, check_vma=False
    )
```

profile of v0, /device:TPU:0, one launch (start us, length us, event | category | flops | bytes accessed | tf_op | source)
XLA Modules:
  0.0 237.8 jit_solution(1407843614711286646)
XLA Ops:
  7.3 1.5 copy-done
  8.8 5.2 %convolution_multiply_fusion = f32[512,128]{1,0:T(8,128)} fusion(f32[1024,512]{1,0:T(8,128)S(1)} %copy-done, f32[1024,128]{1,0:T(8,128)} %param.7), kind=kOutput, calls=%fused_computation.1 | convolution fusion | flops 805371904 | bytes 2883584 | tf_op jit(solution)/shard_map/dot_general | solution.py:12
  14.0 2.5 %convolution_multiply_fusion.1 = f32[512,128]{1,0:T(8,128)} fusion(f32[512,512]{1,0:T(8,128)S(1)} %copy-done.1, f32[512,128]{1,0:T(8,128)S(1)} %copy-done.4), kind=kOutput, calls=%fused_computation.3 | convolution fusion | flops 402718720 | bytes 1572864 | tf_op jit(solution)/shard_map/dot_general | solution.py:12
  16.6 0.8 copy.9
  17.4 53.3 %all-reduce.5.cloned.1.call-done = f32[512,128]{1,0:T(8,128)} async-done(((f32[512,128]{1,0:T(8,128)}), f32[512,128]{1,0:T(8,128)}) %all-reduce.5.cloned.1.call-update) | async-done | bytes 262160 | tf_op jit(solution)/shard_map/psum | solution.py:31
  70.7 3.4 %abs_reduce_fusion.1 = (f32[]{:T(128)}, f32[128,512]{1,0:T(8,128)}) fusion(f32[128]{0:T(128)S(1)} %copy-done.5, f32[512,128]{1,0:T(8,128)} %all-reduce.5.cloned.1.call-done, f32[512,512]{1,0:T(8,128)S(1)} %copy-done.1), kind=kOutput, calls=%fused_computation.22 | convolution fusion | flops 402849792 | bytes 1573380 | tf_op jit(solution)/shard_map/dot_general | solution.py:34
  74.1 34.3 %all-reduce.3.cloned.1.call-done = f32[512,128]{1,0:T(8,128)} async-done(((f32[512,128]{1,0:T(8,128)}), f32[512,128]{1,0:T(8,128)}) %all-reduce.3.cloned.1.call-update) | async-done | bytes 262160 | tf_op jit(solution)/shard_map/psum | solution.py:32
  108.4 4.2 %abs_reduce_fusion = (f32[]{:T(128)}, f32[128,1024]{1,0:T(8,128)}) fusion(f32[128]{0:T(128)S(1)} %copy-done.5, f32[512,128]{1,0:T(8,128)} %all-reduce.3.cloned.1.call-done, f32[1024,512]{1,0:T(8,128)S(1)} %copy-done), kind=kOutput, calls=%fused_computation.18 | convolution fusion | flops 805699584 | bytes 2884100 | tf_op jit(solution)/shard_map/dot_general | solution.py:33
  114.2 40.2 %pmax.7 = f32[]{:T(128)} all-reduce(f32[]{:T(128)S(6)} %max.8), channel_id=1, replica_groups=mesh['cand'=8,'ref'=4] {'cand','ref'}, use_global_device_ids=true, to_apply=%region_4.0 | all-reduce | flops 1 | bytes 8 | tf_op jit(solution)/shard_map/pmax | solution.py:37
  154.4 1.0 multiply_reduce_fusion
  155.4 0.6 abs_reduce_fusion.2
  157.3 1.1 bitcast_multiply_fusion.1
  158.7 0.3 fusion
  158.9 10.4 %psum.59 = f32[128]{0:T(128)S(1)} all-reduce(f32[128]{0:T(128)S(1)} %fusion), channel_id=1, replica_groups=mesh['cand'=8,'ref'=4] {'ref'}, use_global_device_ids=true, to_apply=%region_8.0 | all-reduce | flops 128 | bytes 1024 | tf_op jit(solution)/shard_map/psum | solution.py:52
  169.4 1.1 bitcast_multiply_fusion
  170.5 0.4 fusion.16
  170.9 0.5 fusion.5
  171.4 11.8 %psum.58 = f32[128]{0:T(128)S(1)} all-reduce(f32[128]{0:T(128)S(1)} %fusion.5), channel_id=1, replica_groups=mesh['cand'=8,'ref'=4] {'cand'}, use_global_device_ids=true, to_apply=%region_7.0 | all-reduce | flops 128 | bytes 1024 | tf_op jit(solution)/shard_map/psum | solution.py:51
  183.2 0.3 fusion.10
  183.5 0.4 fusion.12
  183.9 0.3 fusion.1
  184.2 8.4 %psum.61 = f32[128]{0:T(128)S(1)} all-reduce(f32[128]{0:T(128)S(1)} %fusion.1), channel_id=1, replica_groups=mesh['cand'=8,'ref'=4] {'ref'}, use_global_device_ids=true, to_apply=%region_10.0 | all-reduce | flops 128 | bytes 1024 | tf_op jit(solution)/shard_map/psum | solution.py:52
  192.6 0.5 fusion.4
  193.1 11.8 %psum.60 = f32[128]{0:T(128)S(1)} all-reduce(f32[128]{0:T(128)S(1)} %fusion.4), channel_id=1, replica_groups=mesh['cand'=8,'ref'=4] {'cand'}, use_global_device_ids=true, to_apply=%region_9.0 | all-reduce | flops 128 | bytes 1024 | tf_op jit(solution)/shard_map/psum | solution.py:51
  205.0 0.4 fusion.8
  205.4 0.5 fusion.3
  205.9 12.1 %psum.62 = f32[128]{0:T(128)S(1)} all-reduce(f32[128]{0:T(128)S(1)} %fusion.3), channel_id=1, replica_groups=mesh['cand'=8,'ref'=4] {'cand'}, use_global_device_ids=true, to_apply=%region_11.0 | all-reduce | flops 128 | bytes 1024 | tf_op jit(solution)/shard_map/psum | solution.py:51
  217.9 0.3 fusion.6
  218.2 0.3 fusion.2
  218.5 10.4 %psum.63 = f32[128]{0:T(128)S(1)} all-reduce(f32[128]{0:T(128)S(1)} %fusion.2), channel_id=1, replica_groups=mesh['cand'=8,'ref'=4] {'ref'}, use_global_device_ids=true, to_apply=%region_12.0 | all-reduce | flops 128 | bytes 1024 | tf_op jit(solution)/shard_map/psum | solution.py:52
  229.0 0.8 copy.11
  230.0 1.0 copy.10
  (32 shorter events, 0.9 us)
Async XLA Ops:
  7.2 1.6 copy-start
  7.2 6.8 %copy-start.1 = (f32[512,512]{1,0:T(8,128)S(1)}, f32[512,512]{1,0:T(8,128)}, u32[]{:S(2)}) copy-start(f32[512,512]{1,0:T(8,128)} %param.6) | copy-start | bytes 3145732
  7.2 6.8 %copy-start.4 = (f32[512,128]{1,0:T(8,128)S(1)}, f32[512,128]{1,0:T(8,128)}, u32[]{:S(2)}) copy-start(f32[512,128]{1,0:T(8,128)} %param.8) | copy-start | bytes 786436
  7.2 63.5 %copy-start.5 = (f32[128]{0:T(128)S(1)}, f32[128]{0:T(128)}, u32[]{:S(2)}) copy-start(f32[128]{0:T(128)} %param.9) | copy-start | bytes 1540
  7.2 63.5 %all-reduce.5.cloned.1.call-start = ((), (), s32[]{:S(2)}) async-start(), calls=%async_computation.1 | async-start | bytes 524288 | tf_op jit(solution)/shard_map/psum | solution.py:31
  14.0 94.5 %all-reduce.3.cloned.1.call-start = ((), (), s32[]{:S(2)}) async-start(), calls=%async_computation | async-start | bytes 524288 | tf_op jit(solution)/shard_map/psum | solution.py:32
  74.1 39.9 %copy-start.2 = (f32[1024,128]{1,0:T(8,128)S(1)}, f32[1024,128]{1,0:T(8,128)}, u32[]{:S(2)}) copy-start(f32[1024,128]{1,0:T(8,128)} %param.7) | copy-start | bytes 1572868
  74.1 80.3 %copy-start.3 = (f32[512,128]{1,0:T(8,128)S(1)}, f32[512,128]{1,0:T(8,128)}, u32[]{:S(2)}) copy-start(f32[512,128]{1,0:T(8,128)} %all-reduce.5.cloned.1.call-done) | copy-start | bytes 786436
  228.9 2.1 copy-start.6
Sparse Core Ops, SparseCore 0:
  14.1 56.5 all-reduce.4
  73.6 34.7 all-reduce.2
where the time goes:
time: 238 us
  blocking collectives  105 us (44%)
  waiting for transfers between devices  87.7 us (37%)
  matrix products  19.6 us (8%)
  between operations  16.8 us (7%)
  local copies, waits for them, and re-layouts  4.4 us (2%)
  other arithmetic  4.18 us (2%)
    psum x1, waiting for transfers between devices, on_device(): cand_moment = lax.psum(cand_partial, 'cand')  53.3 us
    pmax x1, blocking collectives, on_device(): global_top = lax.pmax(local_top, ('cand', 'ref'))  40.2 us
    psum x3, blocking collectives, on_device(): mass_cand = lax.psum(cand_mass_part, 'cand')  35.7 us
    psum x1, waiting for transfers between devices, on_device(): ref_moment = lax.psum(ref_partial, 'ref')  34.3 us
    psum x3, blocking collectives, on_device(): mass_ref = lax.psum(ref_mass_part, 'ref')  29.3 us
    dot_general x2, matrix products, contract_rows(): lax.dot_general(left, right, (((0,), (0,)), ((), ())), precision=lax.Prec...  7.68 us
  transfers between devices with their start and end apart: 2, of which 2 were waited for; matrix products, arithmetic and copies ran while one was open for 3% of the time, Pallas kernels for 0%

commit v1 on v0

--- a/solution.py
+++ b/solution.py
@@ -28,7 +28,8 @@
     ref_block, ref_local = (ref_factor, ref_plan)
     cand_partial = contract_rows(cand_block, cand_local) / cand_total
     ref_partial = contract_rows(ref_block, ref_local) / ref_total
-    cand_moment = lax.psum(cand_partial, "cand")
+    parts = lax.all_gather(cand_partial, "cand")
+    cand_moment = jnp.sum(parts, axis=0)
     ref_moment = lax.psum(ref_partial, "ref")
     grad_cand = jnp.dot(cand_block, ref_moment, precision=lax.Precision.HIGHEST) / weights[None, :]
     grad_ref = jnp.dot(ref_block, cand_moment, precision=lax.Precision.HIGHEST) / weights[None, :]

time: 238 us -> 185 us (0.78)
  waiting for transfers between devices: 87.7 us -> 32.4 us
    psum x1 -> x0, waiting for transfers between devices: 53.3 us -> none  [on_device(): cand_moment = lax.psum(cand_partial, 'cand')]
  transfers between devices with their start and end apart: 2 -> 2, of which waited for: 2 -> 1; matrix products, arithmetic and copies ran while one was open for 3% -> 6% of each run, Pallas kernels for 0% -> 0%
where the time goes in v1:
time: 185 us; the launch traced here: 184 us
  blocking collectives  105 us (57%)
  waiting for transfers between devices  32.4 us (18%)
  matrix products  19 us (10%)
  between operations  18.2 us (10%)
  other arithmetic  6.07 us (3%)
  local copies, waits for them, and re-layouts  3.71 us (2%)
    pmax x1, blocking collectives, on_device(): global_top = lax.pmax(local_top, ('cand', 'ref'))  40.2 us
    psum x3, blocking collectives, on_device(): mass_cand = lax.psum(cand_mass_part, 'cand')  35.4 us
    psum x1, waiting for transfers between devices, on_device(): ref_moment = lax.psum(ref_partial, 'ref')  32.4 us
    psum x3, blocking collectives, on_device(): mass_ref = lax.psum(ref_mass_part, 'ref')  29.2 us
    dot_general x2, matrix products, contract_rows(): lax.dot_general(left, right, (((0,), (0,)), ((), ())), precision=lax.Prec...  8.07 us
    dot_general x1, matrix products, on_device(): jnp.dot(cand_block, ref_moment, precision=lax.Precision.HIGHEST)  4.22 us
    unnamed x16, local copies, waits for them, and re-layouts  3.71 us
  transfers between devices with their start and end apart: 2, of which 1 were waited for; matrix products, arithmetic and copies ran while one was open for 6% of the time, Pallas kernels for 0%

profile of v1, /device:TPU:0, one launch (start us, length us, event | category | flops | bytes accessed | tf_op | source)
XLA Modules:
  0.0 184.2 jit_solution(7872237270090756091)
XLA Ops:
  8.1 3.9 %convolution_multiply_fusion.1 = f32[512,128]{1,0:T(8,128)} fusion(f32[512,512]{1,0:T(8,128)} %param.6, f32[512,128]{1,0:T(8,128)} %param.8), kind=kOutput, calls=%fused_computation.3 | convolution fusion | flops 402718720 | bytes 1572864 | tf_op jit(solution)/shard_map/dot_general | solution.py:12
  12.1 4.1 %convolution_multiply_fusion = f32[512,128]{1,0:T(8,128)} fusion(f32[1024,512]{1,0:T(8,128)S(1)} %copy-done, f32[1024,128]{1,0:T(8,128)S(1)} %copy-done.2), kind=kOutput, calls=%fused_computation.1 | convolution fusion | flops 805371904 | bytes 2883584 | tf_op jit(solution)/shard_map/dot_general | solution.py:12
  16.3 0.9 copy.9
  17.1 1.0 copy.8
  18.1 32.4 %all-reduce.2.cloned.1.call-done = f32[512,128]{1,0:T(8,128)} async-done(((f32[512,128]{1,0:T(8,128)}), f32[512,128]{1,0:T(8,128)}) %all-reduce.2.cloned.1.call-update) | async-done | bytes 262160 | tf_op jit(solution)/shard_map/psum | solution.py:33
  50.5 4.2 %abs_reduce_fusion = (f32[]{:T(128)}, f32[128,1024]{1,0:T(8,128)}) fusion(f32[128]{0:T(128)S(1)} %copy-done.4, f32[512,128]{1,0:T(8,128)} %all-reduce.2.cloned.1.call-done, f32[1024,512]{1,0:T(8,128)S(1)} %copy-done), kind=kOutput, calls=%fused_computation.18 | convolution fusion | flops 805699584 | bytes 2884100 | tf_op jit(solution)/shard_map/dot_general | solution.py:34
  54.7 1.7 reduce_sum.18
  56.5 2.4 %abs_reduce_fusion.1 = (f32[]{:T(128)}, f32[128,512]{1,0:T(8,128)}) fusion(f32[128]{0:T(128)S(1)} %copy-done.4, f32[512,128]{1,0:T(8,128)S(1)} %reduce_sum.18, f32[512,512]{1,0:T(8,128)S(1)} %copy-done.1), kind=kOutput, calls=%fused_computation.22 | convolution fusion | flops 402849792 | bytes 1573380 | tf_op jit(solution)/shard_map/dot_general | solution.py:35
  60.2 1.0 multiply_reduce_fusion
  61.2 0.6 abs_reduce_fusion.2
  61.9 40.2 %pmax.7 = f32[]{:T(128)} all-reduce(f32[]{:T(128)S(6)} %max.8), channel_id=1, replica_groups=mesh['cand'=8,'ref'=4] {'cand','ref'}, use_global_device_ids=true, to_apply=%region_4.0 | all-reduce | flops 1 | bytes 8 | tf_op jit(solution)/shard_map/pmax | solution.py:38
  103.3 1.1 bitcast_multiply_fusion.1
  104.7 0.3 fusion
  104.9 10.4 %psum.51 = f32[128]{0:T(128)S(1)} all-reduce(f32[128]{0:T(128)S(1)} %fusion), channel_id=1, replica_groups=mesh['cand'=8,'ref'=4] {'ref'}, use_global_device_ids=true, to_apply=%region_8.0 | all-reduce | flops 128 | bytes 1024 | tf_op jit(solution)/shard_map/psum | solution.py:53
  115.3 1.3 bitcast_multiply_fusion
  116.6 0.4 fusion.16
  117.0 0.5 fusion.5
  117.5 11.8 %psum.50 = f32[128]{0:T(128)S(1)} all-reduce(f32[128]{0:T(128)S(1)} %fusion.5), channel_id=1, replica_groups=mesh['cand'=8,'ref'=4] {'cand'}, use_global_device_ids=true, to_apply=%region_7.0 | all-reduce | flops 128 | bytes 1024 | tf_op jit(solution)/shard_map/psum | solution.py:52
  129.3 0.3 fusion.10
  129.6 0.4 fusion.12
  130.0 0.3 fusion.1
  130.3 8.4 %psum.53 = f32[128]{0:T(128)S(1)} all-reduce(f32[128]{0:T(128)S(1)} %fusion.1), channel_id=1, replica_groups=mesh['cand'=8,'ref'=4] {'ref'}, use_global_device_ids=true, to_apply=%region_10.0 | all-reduce | flops 128 | bytes 1024 | tf_op jit(solution)/shard_map/psum | solution.py:53
  138.7 0.5 fusion.4
  139.2 11.8 %psum.52 = f32[128]{0:T(128)S(1)} all-reduce(f32[128]{0:T(128)S(1)} %fusion.4), channel_id=1, replica_groups=mesh['cand'=8,'ref'=4] {'cand'}, use_global_device_ids=true, to_apply=%region_9.0 | all-reduce | flops 128 | bytes 1024 | tf_op jit(solution)/shard_map/psum | solution.py:52
  151.1 0.3 fusion.6
  151.3 0.3 fusion.2
  151.6 10.4 %psum.55 = f32[128]{0:T(128)S(1)} all-reduce(f32[128]{0:T(128)S(1)} %fusion.2), channel_id=1, replica_groups=mesh['cand'=8,'ref'=4] {'ref'}, use_global_device_ids=true, to_apply=%region_12.0 | all-reduce | flops 128 | bytes 1024 | tf_op jit(solution)/shard_map/psum | solution.py:53
  162.0 0.4 fusion.8
  162.4 0.5 fusion.3
  162.9 11.8 %psum.54 = f32[128]{0:T(128)S(1)} all-reduce(f32[128]{0:T(128)S(1)} %fusion.3), channel_id=1, replica_groups=mesh['cand'=8,'ref'=4] {'cand'}, use_global_device_ids=true, to_apply=%region_11.0 | all-reduce | flops 128 | bytes 1024 | tf_op jit(solution)/shard_map/psum | solution.py:52
  174.9 0.8 copy.11
  175.8 1.0 copy.10
  (31 shorter events, 0.7 us)
Async XLA Ops:
  8.0 4.1 %copy-start = (f32[1024,512]{1,0:T(8,128)S(1)}, f32[1024,512]{1,0:T(8,128)}, u32[]{:S(2)}) copy-start(f32[1024,512]{1,0:T(8,128)} %param.5) | copy-start | bytes 6291460
  8.0 4.1 %copy-start.2 = (f32[1024,128]{1,0:T(8,128)S(1)}, f32[1024,128]{1,0:T(8,128)}, u32[]{:S(2)}) copy-start(f32[1024,128]{1,0:T(8,128)} %param.7) | copy-start | bytes 1572868
  8.0 42.5 %all-reduce.2.cloned.1.call-start = ((), (), s32[]{:S(2)}) async-start(), calls=%async_computation | async-start | bytes 524288 | tf_op jit(solution)/shard_map/psum | solution.py:33
  12.0 4.3 %copy-start.3 = (f32[512,128]{1,0:T(8,128)S(1)}, f32[512,128]{1,0:T(8,128)}, u32[]{:S(2)}) copy-start(f32[512,128]{1,0:T(8,128)} %param.8) | copy-start | bytes 786436
  12.0 38.5 %copy-start.4 = (f32[128]{0:T(128)S(1)}, f32[128]{0:T(128)}, u32[]{:S(2)}) copy-start(f32[128]{0:T(128)} %param.9) | copy-start | bytes 1540
  12.0 42.7 %all-gather.3.cloned.1.call-start = ((), (), s32[]{:S(2)}) async-start(), calls=%async_computation.1 | async-start | bytes 2359296 | tf_op jit(solution)/shard_map/all_gather | solution.py:31
  18.1 38.3 %copy-start.1 = (f32[512,512]{1,0:T(8,128)S(1)}, f32[512,512]{1,0:T(8,128)}, u32[]{:S(2)}) copy-start(f32[512,512]{1,0:T(8,128)} %param.6) | copy-start | bytes 3145732
  174.7 2.1 %copy-start.5 = (f32[128]{0:T(128)}, f32[128]{0:T(128)S(1)}, u32[]{:S(2)}) copy-start(f32[128]{0:T(128)S(1)} %get-tuple-element.7) | copy-start | bytes 1540
Sparse Core Ops, SparseCore 0:
  12.1 38.3 all-reduce.1
Sparse Core Ops, SparseCore 1:
  16.4 30.4 all-gather.2
